TPU v7x, 32 devices: a whole 2x2x4 slice. The times are simulated.
32 devices in a mesh: walk: 8 (over y, x, core), par: 4 (over z).
Axes of the slice: x: 2, y: 2, z: 4, core: 2. Of those that a mesh axis runs over, the one named last changes fastest.
Arguments:
- features: bfloat16 [1536, 32, 256], P(('walk', 'par')), may hold values from -6 to 6
- signals: bfloat16 [1536, 32, 256], P(('walk', 'par')), may hold values from -6 to 6
- param_scale: float32 [256, 256], replicated, may hold values from 0.2 to 2
- geometry: int32 [1536], replicated, may hold values from 0 to 63
- electrons: int32 [64], replicated, may hold values from 16 to 32
Outputs:
- panel: float32 [1536, 256], P('walk')
- trailing: float32 [1536, 1536], P('walk', 'par')
All inputs are finite; a program needn't handle non-finite values.
Results may differ from a plain program's by a relative error of at most 0.0003.
Values sent between devices are 32-bit elements; how exact they have to be, the bound alone decides.
No kernel may reach another device: no remote copies, remote signals or barrier semaphores. Data moves between devices by JAX's collectives and lax.ppermute only.
A program may use at most 256 MiB of HBM per device.

v0:
```python
import math
import jax
import jax.numpy as jnp
from jax import lax
from jax.sharding import PartitionSpec as P

PB = 256
HIGHEST = lax.Precision.HIGHEST
SHIFT = 0.05
CONTRACT_LAST = (((1,), (1,)), ((), ()))
CONTRACT_FIRST = (((0,), (0,)), ((), ()))


def outer_rows(left_rows, right_rows):
    return lax.dot_general(left_rows, right_rows, CONTRACT_LAST, precision=HIGHEST)


def first_dims(left_rows, right_rows):
    return lax.dot_general(left_rows, right_rows, CONTRACT_FIRST, precision=HIGHEST)


def one_hot(labels, groups):
    return (labels[:, None] == jnp.arange(groups, dtype=jnp.int32)[None, :]).astype(jnp.float32)


def on_device(features, signals, param_scale, geometry, electrons):
    par_size = lax.axis_size("par")
    walk_index = lax.axis_index("walk")
    par_index = lax.axis_index("par")
    per_device = features.shape[0]
    walkers = geometry.shape[0]
    groups = electrons.shape[0]
    row_block = per_device * par_size
    col_block = walkers // par_size
    width = param_scale.shape[0]
    slots_count = features.shape[1]
    anchor = (walk_index * par_size + par_index) * per_device
    own_geometry = lax.dynamic_slice_in_dim(geometry, anchor, per_device)
    own_matches = own_geometry[:, None] == jnp.arange(groups, dtype=jnp.int32)[None, :]
    own_electrons = jnp.sum(jnp.where(own_matches, electrons[None, :], 0), axis=1)
    live = (jnp.arange(slots_count, dtype=jnp.int32)[None, :] < own_electrons[:, None]).astype(
        features.dtype
    )
    masked = features * live[:, :, None]
    scaling = param_scale * (1.0 / math.sqrt(slots_count * width * width))
    jacobian = (
        jnp.einsum("wei,wej->wij", masked, signals, preferred_element_type=jnp.float32)
        * scaling[None]
    )
    jacobian = jacobian.reshape(per_device, width * width)
    all_onehot = one_hot(geometry, groups)
    counts = jnp.maximum(jnp.sum(all_onehot, axis=0), 1.0)
    reciprocal = 1.0 / counts
    columns = lax.all_to_all(jacobian, ("walk", "par"), split_axis=1, concat_axis=0, tiled=True)
    sums = first_dims(all_onehot, columns)
    columns = columns - jnp.dot(all_onehot, sums * reciprocal[:, None], precision=HIGHEST)
    stripe = lax.psum_scatter(outer_rows(columns, columns), "walk", scatter_dimension=0, tiled=True)
    gram = lax.psum_scatter(stripe, "par", scatter_dimension=1, tiled=True)
    row_ids = walk_index * row_block + jnp.arange(row_block, dtype=jnp.int32)
    col_ids = par_index * col_block + jnp.arange(col_block, dtype=jnp.int32)
    shifted = gram + SHIFT * (row_ids[:, None] == col_ids[None, :]).astype(jnp.float32)
    whole_rows = lax.all_gather(shifted, "par", axis=1, tiled=True)
    panel_part = whole_rows[:, :PB]
    panel_whole = lax.all_gather(panel_part, "walk", axis=0, tiled=True)
    factor_head = jnp.linalg.cholesky(panel_whole[:PB])
    head_inverse = jax.scipy.linalg.solve_triangular(
        factor_head, jnp.eye(PB, dtype=jnp.float32), lower=True
    )
    own_panel = outer_rows(panel_part, head_inverse)
    col_rows = lax.dynamic_slice_in_dim(panel_whole, par_index * col_block, col_block, 0)
    col_panel = outer_rows(col_rows, head_inverse)
    trailing = shifted - outer_rows(own_panel, col_panel)
    return (own_panel, trailing)


def solution(mesh):
    in_specs = (P(("walk", "par"), None, None), P(("walk", "par"), None, None), P(), P(), P())
    out_specs = (P("walk", None), P("walk", "par"))
    return jax.shard_map(
        on_device, mesh=mesh, in_specs=in_specs, out_specs=out_specs, check_vma=False
    )
```

profile of v0, /device:TPU:0, one launch (start us, length us, event | category | flops | bytes accessed | tf_op | source)
XLA Modules:
  0.0 659.6 jit_solution(1431024369149093980)
XLA Ops:
  9.9 8.6 %broadcast_multiply_fusion = f32[48,256,256]{2,1,0:T(8,128)} fusion(f32[256,256]{1,0:T(8,128)S(1)} %broadcast_multiply_fusion.1, bf16[48,32,256]{2,1,0:T(8,128)(2,1)S(1)} %copy-done, bf16[48,32,256]{2,1,0:T(8,128)(2,1)} %param.5, bf16[48,32]{1,0:T(8,128)(2,1)S(1)} %fusion.18), kind=kOutput, calls=%fused_computation.4 | convolution fusion | flops 204865536 | bytes 14420992 | tf_op jit(solution)/shard_map/wei,wej->wij/dot_general | solution.py:47
  18.6 13.6 %all_to_all.14 = f32[48,32,2048]{2,1,0:T(8,128)} reshape(f32[48,256,256]{2,1,0:T(8,128)} %broadcast_multiply_fusion) | data formatting | bytes 25165824 | tf_op jit(solution)/shard_map/all_to_all | solution.py:54
  32.2 16.3 %copy.21 = f32[48,32,2048]{2,0,1:T(8,128)} copy(f32[48,32,2048]{2,1,0:T(8,128)} %all_to_all.14) | data formatting | bytes 25165824 | tf_op jit(solution)/shard_map/all_to_all | solution.py:54
  48.5 7.4 %all-to-all-start = ((f32[48,32,2048]{2,0,1:T(8,128)}), f32[48,32,2048]{2,0,1:T(8,128)}, u32[]{:S(2)}, u32[]{:S(2)}) async-start(f32[48,32,2048]{2,0,1:T(8,128)} %copy.21), calls=%async_computation | async-start | bytes 25165824 | tf_op jit(solution)/shard_map/all_to_all | solution.py:54
  56.6 270.2 %all-to-all-done = f32[48,32,2048]{2,0,1:T(8,128)} async-done(((f32[48,32,2048]{2,0,1:T(8,128)}), f32[48,32,2048]{2,0,1:T(8,128)}, u32[]{:S(2)}, u32[]{:S(2)}) %all-to-all-start) | async-done | bytes 12582944 | tf_op jit(solution)/shard_map/all_to_all | solution.py:54
  326.8 7.9 %convolution_multiply_fusion = f32[64,2048]{1,0:T(8,128)S(1)} fusion(f32[1536,2048]{1,0:T(8,128)} %bitcast.1, f32[64]{0:T(128)S(1)} %maximum_divide_fusion, s32[1536]{0:T(1024)S(1)} %copy-done.3), kind=kOutput, calls=%fused_computation.5 | convolution fusion | flops 2416148480 | bytes 13113600 | tf_op jit(solution)/shard_map/dot_general | solution.py:19
  334.7 8.1 %fusion.5 = f32[1536,2048]{1,0:T(8,128)} fusion(f32[64,2048]{1,0:T(8,128)S(1)} %convolution_multiply_fusion, s32[1536]{0:T(1024)S(1)} %copy-done.3), kind=kOutput, calls=%fused_computation.14 | convolution fusion | flops 2416017408 | bytes 13113344 | tf_op jit(solution)/shard_map/dot_general | solution.py:56
  342.8 69.0 %fusion = f32[1536,1536]{1,0:T(8,128)} fusion(f32[1536,2048]{1,0:T(8,128)} %bitcast.1, f32[1536,2048]{1,0:T(8,128)} %fusion.5), kind=kOutput, calls=%fused_computation.2 | convolution fusion | flops 57985204224 | bytes 34603008
  411.9 83.2 %reduce-scatter.7.cloned.1.call-done = f32[192,1536]{1,0:T(8,128)} async-done(((f32[1536,1536]{1,0:T(8,128)}), f32[192,1536]{1,0:T(8,128)}) %reduce-scatter.7.cloned.1.call-update) | async-done | bytes 1179664 | tf_op jit(solution)/shard_map/reduce_scatter | solution.py:57
  495.2 31.4 %reduce-scatter.5.cloned.1.call-done = f32[192,384]{1,0:T(8,128)} async-done(((f32[192,1536]{1,0:T(8,128)}), f32[192,384]{1,0:T(8,128)}) %reduce-scatter.5.cloned.1.call-update) | async-done | bytes 294928 | tf_op jit(solution)/shard_map/reduce_scatter | solution.py:58
  526.6 1.8 select_add_fusion
  528.7 29.3 %all-gather.3.cloned.1.call-done = f32[192,1536]{1,0:T(8,128)} async-done(((f32[192,384]{1,0:T(8,128)}), f32[192,1536]{1,0:T(8,128)}) %all-gather.3.cloned.1.call-update) | async-done | bytes 1179664 | tf_op jit(solution)/shard_map/all_gather | solution.py:62
  558.0 1.6 slice.67
  559.7 25.5 %all-gather.5.cloned.1.call-done = f32[1536,256]{1,0:T(8,128)} async-done(((f32[192,256]{1,0:T(8,128)}), f32[1536,256]{1,0:T(8,128)}) %all-gather.5.cloned.1.call-update) | async-done | bytes 1572880 | tf_op jit(solution)/shard_map/all_gather | solution.py:64
  587.2 11.7 %cholesky.50 = f32[128,128]{1,0:T(8,128)S(1)} custom-call(f32[128,128]{1,0:T(8,128)S(1)} %cholesky.118), custom_call_target="Cholesky" | custom-call | tf_op jit(solution)/shard_map/jit(cholesky)/cholesky | solution.py:65
  599.0 9.8 %custom-call.15 = f32[1,128,128]{1,2,0:T(8,128)S(1)} custom-call(f32[1,128,128]{2,1,0:T(8,128)S(1)} %get-tuple-element.27), custom_call_target="InvertDiagBlocksLowerTriangular" | custom-call | tf_op jit(solution)/shard_map/jit(cholesky)/cholesky | solution.py:65
  609.3 11.7 %cholesky.105 = f32[128,128]{1,0:T(8,128)S(1)} custom-call(f32[128,128]{1,0:T(8,128)S(1)} %convolution_subtract_fusion.2), custom_call_target="Cholesky" | custom-call | tf_op jit(solution)/shard_map/jit(cholesky)/cholesky | solution.py:65
  623.1 4.0 while.1
  623.9 1.3 bitcast_dynamic-update-slice_fusion.2
  625.8 1.3 bitcast_dynamic-update-slice_fusion.2
  627.1 19.7 %custom-call.16 = f32[2,128,128]{1,2,0:T(8,128)S(1)} custom-call(f32[2,128,128]{2,1,0:T(8,128)S(1)} %get-tuple-element.9), custom_call_target="InvertDiagBlocksLowerTriangular" | custom-call | tf_op jit(solution)/shard_map/jit(_solve_triangular)/triangular_solve | solution.py:66
  647.6 1.4 fusion.8
  649.0 1.6 fusion.3
  650.6 2.2 convolution_subtract_fusion
  (46 shorter events, 9.2 us)
Async XLA Ops:
  7.2 2.8 copy-start
  48.5 7.9 %copy-start.3 = (s32[1536]{0:T(1024)S(1)}, s32[1536]{0:T(1024)}, u32[]{:S(2)}) copy-start(s32[1536]{0:T(1024)} %param.8) | copy-start | bytes 18436
  48.5 278.3 %all-to-all-start = ((f32[48,32,2048]{2,0,1:T(8,128)}), f32[48,32,2048]{2,0,1:T(8,128)}, u32[]{:S(2)}, u32[]{:S(2)}) async-start(f32[48,32,2048]{2,0,1:T(8,128)} %copy.21), calls=%async_computation | async-start | bytes 25165824 | tf_op jit(solution)/shard_map/all_to_all | solution.py:54
  55.9 439.2 %reduce-scatter.7.cloned.1.call-start = ((), (), s32[]{:S(2)}) async-start(), calls=%async_computation.6 | async-start | bytes 10616832 | tf_op jit(solution)/shard_map/reduce_scatter | solution.py:57
  342.8 310.0 %copy-start.1 = (bf16[48,32,256]{2,1,0:T(8,128)(2,1)S(1)}, bf16[48,32,256]{2,1,0:T(8,128)(2,1)}, u32[]{:S(2)}) copy-start(bf16[48,32,256]{2,1,0:T(8,128)(2,1)} %param.6) | copy-start | bytes 2359300
  411.8 114.8 %reduce-scatter.5.cloned.1.call-start = ((), (), s32[]{:S(2)}) async-start(), calls=%async_computation.3 | async-start | bytes 1474560 | tf_op jit(solution)/shard_map/reduce_scatter | solution.py:58
  495.1 62.9 %all-gather.3.cloned.1.call-start = ((), (), s32[]{:S(2)}) async-start(), calls=%async_computation.4 | async-start | bytes 1474560 | tf_op jit(solution)/shard_map/all_gather | solution.py:62
  528.4 56.7 %all-gather.5.cloned.1.call-start = ((), (), s32[]{:S(2)}) async-start(), calls=%async_computation.5 | async-start | bytes 1769472 | tf_op jit(solution)/shard_map/all_gather | solution.py:64
  649.0 3.8 copy-start.2
Sparse Core Ops, SparseCore 0:
  412.0 83.0 reduce-scatter.6
  497.4 29.1 reduce-scatter.4
  528.8 29.1 all-gather.2
  560.3 24.7 all-gather.4
where the time goes:
time: 668 us; the launch traced here: 660 us
  waiting for transfers between devices  440 us (66%)
  matrix products  100 us (15%)
  other arithmetic  58.5 us (9%)
  local copies, waits for them, and re-layouts  37.4 us (6%)
  between operations  15.4 us (2%)
  starting transfers between devices  8.2 us (1%)
    all_to_all x1, waiting for transfers between devices, on_device(): lax.all_to_all(jacobian, ('walk', 'par'), split_axis=1, concat_axis=0, ti...  270 us
    reduce_scatter x1, waiting for transfers between devices, on_device(): lax.psum_scatter(outer_rows(columns, columns), 'walk', scatter_dimension=...  83.2 us
    unnamed x1, matrix products  69 us
    another operation x6, other arithmetic, on_device(): factor_head = jnp.linalg.cholesky(panel_whole[:PB])  34 us
    reduce_scatter x1, waiting for transfers between devices, on_device(): gram = lax.psum_scatter(stripe, 'par', scatter_dimension=1, tiled=True)  31.4 us
    all_to_all x2, local copies, waits for them, and re-layouts, on_device(): lax.all_to_all(jacobian, ('walk', 'par'), split_axis=1, concat_axis=0, ti...  29.9 us
    all_gather x1, waiting for transfers between devices, on_device(): whole_rows = lax.all_gather(shifted, 'par', axis=1, tiled=True)  29.3 us
    all_gather x1, waiting for transfers between devices, on_device(): panel_whole = lax.all_gather(panel_part, 'walk', axis=0, tiled=True)  25.5 us
  transfers between devices with their start and end apart: 5, of which 5 were waited for; matrix products, arithmetic and copies ran while one was open for 0% of the time, Pallas kernels for 0%

commit v1 on v0

--- a/solution.py
+++ b/solution.py
@@ -59,7 +59,12 @@
     row_ids = walk_index * row_block + jnp.arange(row_block, dtype=jnp.int32)
     col_ids = par_index * col_block + jnp.arange(col_block, dtype=jnp.int32)
     shifted = gram + SHIFT * (row_ids[:, None] == col_ids[None, :]).astype(jnp.float32)
-    whole_rows = lax.all_gather(shifted, "par", axis=1, tiled=True)
+    ring = [shifted]
+    for hop in range(3):
+        ring.append(lax.ppermute(ring[-1], "par", [(dev, (dev + 1) % 4) for dev in range(4)]))
+    whole_rows = jnp.roll(
+        jnp.concatenate(ring[::-1], axis=1), (lax.axis_index("par") + 1) * ring[0].shape[1], axis=1
+    )
     panel_part = whole_rows[:, :PB]
     panel_whole = lax.all_gather(panel_part, "walk", axis=0, tiled=True)
     factor_head = jnp.linalg.cholesky(panel_whole[:PB])

time: 668 us -> 663 us (level)
    all_gather x1 -> x0, waiting for transfers between devices: 29.3 us -> none  [on_device(): whole_rows = lax.all_gather(shifted, 'par', axis=1, tiled=True)]
    ppermute x0 -> x3, waiting for transfers between devices: none -> 28.4 us  [on_device(): lax.ppermute(ring[-1], 'par', [(dev, (dev + 1) % 4) for dev in range(4)])]
  transfers between devices with their start and end apart: 5 -> 7, of which waited for: 5 -> 7; matrix products, arithmetic and copies ran while one was open for 0% -> 0% of each run, Pallas kernels for 0% -> 0%
where the time goes in v1:
time: 663 us; the launch traced here: 654 us
  waiting for transfers between devices  437 us (66%)
  matrix products  98.1 us (15%)
  other arithmetic  58.1 us (9%)
  local copies, waits for them, and re-layouts  36.8 us (6%)
  between operations  15.5 us (2%)
  starting transfers between devices  8.21 us (1%)
    all_to_all x1, waiting for transfers between devices, on_device(): lax.all_to_all(jacobian, ('walk', 'par'), split_axis=1, concat_axis=0, ti...  270 us
    reduce_scatter x1, waiting for transfers between devices, on_device(): lax.psum_scatter(outer_rows(columns, columns), 'walk', scatter_dimension=...  83.2 us
    unnamed x1, matrix products  68.9 us
    another operation x6, other arithmetic, on_device(): factor_head = jnp.linalg.cholesky(panel_whole[:PB])  34 us
    reduce_scatter x1, waiting for transfers between devices, on_device(): gram = lax.psum_scatter(stripe, 'par', scatter_dimension=1, tiled=True)  31.4 us
    all_to_all x2, local copies, waits for them, and re-layouts, on_device(): lax.all_to_all(jacobian, ('walk', 'par'), split_axis=1, concat_axis=0, ti...  29.9 us
    ppermute x3, waiting for transfers between devices, on_device(): lax.ppermute(ring[-1], 'par', [(dev, (dev + 1) % 4) for dev in range(4)])  28.4 us
    all_gather x1, waiting for transfers between devices, on_device(): panel_whole = lax.all_gather(panel_part, 'walk', axis=0, tiled=True)  23.9 us
  transfers between devices with their start and end apart: 7, of which 7 were waited for; matrix products, arithmetic and copies ran while one was open for 0% of the time, Pallas kernels for 0%

profile of v1, /device:TPU:0, one launch (start us, length us, event | category | flops | bytes accessed | tf_op | source)
XLA Modules:
  0.0 654.3 jit_solution(16636115285721262832)
XLA Ops:
  9.9 8.6 %broadcast_multiply_fusion = f32[48,256,256]{2,1,0:T(8,128)} fusion(f32[256,256]{1,0:T(8,128)S(1)} %broadcast_multiply_fusion.1, bf16[48,32,256]{2,1,0:T(8,128)(2,1)S(1)} %copy-done, bf16[48,32,256]{2,1,0:T(8,128)(2,1)} %param.5, bf16[48,32]{1,0:T(8,128)(2,1)S(1)} %fusion.18), kind=kOutput, calls=%fused_computation.4 | convolution fusion | flops 204865536 | bytes 14420992 | tf_op jit(solution)/shard_map/wei,wej->wij/dot_general | solution.py:47
  18.6 13.6 %all_to_all.14 = f32[48,32,2048]{2,1,0:T(8,128)} reshape(f32[48,256,256]{2,1,0:T(8,128)} %broadcast_multiply_fusion) | data formatting | bytes 25165824 | tf_op jit(solution)/shard_map/all_to_all | solution.py:54
  32.2 16.3 %copy.21 = f32[48,32,2048]{2,0,1:T(8,128)} copy(f32[48,32,2048]{2,1,0:T(8,128)} %all_to_all.14) | data formatting | bytes 25165824 | tf_op jit(solution)/shard_map/all_to_all | solution.py:54
  48.5 7.4 %all-to-all-start = ((f32[48,32,2048]{2,0,1:T(8,128)}), f32[48,32,2048]{2,0,1:T(8,128)}, u32[]{:S(2)}, u32[]{:S(2)}) async-start(f32[48,32,2048]{2,0,1:T(8,128)} %copy.21), calls=%async_computation | async-start | bytes 25165824 | tf_op jit(solution)/shard_map/all_to_all | solution.py:54
  56.6 270.2 %all-to-all-done = f32[48,32,2048]{2,0,1:T(8,128)} async-done(((f32[48,32,2048]{2,0,1:T(8,128)}), f32[48,32,2048]{2,0,1:T(8,128)}, u32[]{:S(2)}, u32[]{:S(2)}) %all-to-all-start) | async-done | bytes 12582944 | tf_op jit(solution)/shard_map/all_to_all | solution.py:54
  326.8 7.9 %convolution_multiply_fusion = f32[64,2048]{1,0:T(8,128)S(1)} fusion(f32[1536,2048]{1,0:T(8,128)} %bitcast.1, f32[64]{0:T(128)S(1)} %maximum_divide_fusion, s32[1536]{0:T(1024)S(1)} %copy-done.5), kind=kOutput, calls=%fused_computation.5 | convolution fusion | flops 2416148480 | bytes 13113600 | tf_op jit(solution)/shard_map/dot_general | solution.py:19
  334.7 8.1 %fusion.5 = f32[1536,2048]{1,0:T(8,128)} fusion(f32[64,2048]{1,0:T(8,128)S(1)} %convolution_multiply_fusion, s32[1536]{0:T(1024)S(1)} %copy-done.5), kind=kOutput, calls=%fused_computation.14 | convolution fusion | flops 2416017408 | bytes 13113344 | tf_op jit(solution)/shard_map/dot_general | solution.py:56
  342.8 68.9 %fusion = f32[1536,1536]{1,0:T(8,128)} fusion(f32[1536,2048]{1,0:T(8,128)} %bitcast.1, f32[1536,2048]{1,0:T(8,128)} %fusion.5), kind=kOutput, calls=%fused_computation.2 | convolution fusion | flops 57985204224 | bytes 34603008
  411.8 83.2 %reduce-scatter.7.cloned.1.call-done = f32[192,1536]{1,0:T(8,128)} async-done(((f32[1536,1536]{1,0:T(8,128)}), f32[192,1536]{1,0:T(8,128)}) %reduce-scatter.7.cloned.1.call-update) | async-done | bytes 1179664 | tf_op jit(solution)/shard_map/reduce_scatter | solution.py:57
  495.1 31.4 %reduce-scatter.5.cloned.1.call-done = f32[192,384]{1,0:T(8,128)} async-done(((f32[192,1536]{1,0:T(8,128)}), f32[192,384]{1,0:T(8,128)}) %reduce-scatter.5.cloned.1.call-update) | async-done | bytes 294928 | tf_op jit(solution)/shard_map/reduce_scatter | solution.py:58
  526.6 1.1 select_add_fusion
  527.8 10.4 %collective-permute-done = f32[192,384]{1,0:T(8,128)S(1)} collective-permute-done((f32[192,384]{1,0:T(8,128)S(1)}, f32[192,384]{1,0:T(8,128)S(1)}, u32[]{:S(2)}, u32[]{:S(2)}) %collective-permute-start) | collective-permute-done | bytes 294944 | tf_op jit(solution)/shard_map/ppermute | solution.py:64
  538.2 9.5 %collective-permute-done.1 = f32[192,384]{1,0:T(8,128)S(1)} collective-permute-done((f32[192,384]{1,0:T(8,128)S(1)}, f32[192,384]{1,0:T(8,128)S(1)}, u32[]{:S(2)}, u32[]{:S(2)}) %collective-permute-start.1) | collective-permute-done | bytes 294944 | tf_op jit(solution)/shard_map/ppermute | solution.py:64
  547.8 8.5 %collective-permute-done.2 = f32[192,384]{1,0:T(8,128)S(1)} collective-permute-done((f32[192,384]{1,0:T(8,128)S(1)}, f32[192,384]{1,0:T(8,128)S(1)}, u32[]{:S(2)}, u32[]{:S(2)}) %collective-permute-start.2) | collective-permute-done | bytes 294944 | tf_op jit(solution)/shard_map/ppermute | solution.py:64
  557.7 23.9 %all-gather.2.cloned.1.call-done = f32[1536,256]{1,0:T(8,128)} async-done(((f32[192,256]{1,0:T(8,128)}), f32[1536,256]{1,0:T(8,128)}) %all-gather.2.cloned.1.call-update) | async-done | bytes 1572880 | tf_op jit(solution)/shard_map/all_gather | solution.py:69
  583.7 11.7 %cholesky.50 = f32[128,128]{1,0:T(8,128)S(1)} custom-call(f32[128,128]{1,0:T(8,128)S(1)} %cholesky.118), custom_call_target="Cholesky" | custom-call | tf_op jit(solution)/shard_map/jit(cholesky)/cholesky | solution.py:70
  595.5 9.8 %custom-call.15 = f32[1,128,128]{1,2,0:T(8,128)S(1)} custom-call(f32[1,128,128]{2,1,0:T(8,128)S(1)} %get-tuple-element.27), custom_call_target="InvertDiagBlocksLowerTriangular" | custom-call | tf_op jit(solution)/shard_map/jit(cholesky)/cholesky | solution.py:70
  605.8 11.7 %cholesky.105 = f32[128,128]{1,0:T(8,128)S(1)} custom-call(f32[128,128]{1,0:T(8,128)S(1)} %convolution_subtract_fusion.2), custom_call_target="Cholesky" | custom-call | tf_op jit(solution)/shard_map/jit(cholesky)/cholesky | solution.py:70
  619.6 4.1 while.1
  620.4 1.3 bitcast_dynamic-update-slice_fusion.2
  622.4 1.3 bitcast_dynamic-update-slice_fusion.2
  623.7 19.7 %custom-call.16 = f32[2,128,128]{1,2,0:T(8,128)S(1)} custom-call(f32[2,128,128]{2,1,0:T(8,128)S(1)} %get-tuple-element.9), custom_call_target="InvertDiagBlocksLowerTriangular" | custom-call | tf_op jit(solution)/shard_map/jit(_solve_triangular)/triangular_solve | solution.py:71
  644.6 1.6 fusion.3
  646.2 1.3 convolution_subtract_fusion
  (61 shorter events, 11.0 us)
Async XLA Ops:
  7.2 2.8 copy-start
  48.5 7.9 %copy-start.5 = (s32[1536]{0:T(1024)S(1)}, s32[1536]{0:T(1024)}, u32[]{:S(2)}) copy-start(s32[1536]{0:T(1024)} %param.8) | copy-start | bytes 18436
  48.5 278.3 %all-to-all-start = ((f32[48,32,2048]{2,0,1:T(8,128)}), f32[48,32,2048]{2,0,1:T(8,128)}, u32[]{:S(2)}, u32[]{:S(2)}) async-start(f32[48,32,2048]{2,0,1:T(8,128)} %copy.21), calls=%async_computation | async-start | bytes 25165824 | tf_op jit(solution)/shard_map/all_to_all | solution.py:54
  55.9 439.1 %reduce-scatter.7.cloned.1.call-start = ((), (), s32[]{:S(2)}) async-start(), calls=%async_computation.5 | async-start | bytes 10616832 | tf_op jit(solution)/shard_map/reduce_scatter | solution.py:57
  411.8 114.8 %reduce-scatter.5.cloned.1.call-start = ((), (), s32[]{:S(2)}) async-start(), calls=%async_computation.3 | async-start | bytes 1474560 | tf_op jit(solution)/shard_map/reduce_scatter | solution.py:58
  495.1 86.5 %all-gather.2.cloned.1.call-start = ((), (), s32[]{:S(2)}) async-start(), calls=%async_computation.4 | async-start | bytes 1769472 | tf_op jit(solution)/shard_map/all_gather | solution.py:69
  526.6 29.9 %copy-start.2 = (f32[192,384]{1,0:T(8,128)S(1)}, f32[192,384]{1,0:T(8,128)}, u32[]{:S(2)}) copy-start(f32[192,384]{1,0:T(8,128)} %reduce-scatter.5.cloned.1.call-done) | copy-start | bytes 884740
  527.7 10.4 %collective-permute-start = (f32[192,384]{1,0:T(8,128)S(1)}, f32[192,384]{1,0:T(8,128)S(1)}, u32[]{:S(2)}, u32[]{:S(2)}) collective-permute-start(f32[192,384]{1,0:T(8,128)S(1)} %select_add_fusion), channel_id=1, source_target_pairs={{0,1},{1,2},{2,3},{3,0},{4,5},{5,6},{6,7},{7,4},{8,9},{9,10},{10,1... | collective-permute-start | bytes 884744 | tf_op jit(solution)/shard_map/ppermute | solution.py:64
  538.2 9.5 %collective-permute-start.1 = (f32[192,384]{1,0:T(8,128)S(1)}, f32[192,384]{1,0:T(8,128)S(1)}, u32[]{:S(2)}, u32[]{:S(2)}) collective-permute-start(f32[192,384]{1,0:T(8,128)S(1)} %collective-permute-done), channel_id=1, source_target_pairs={{0,1},{1,2},{2,3},{3,0},{4,5},{5,6},{6,7},{7,4},{8,9},{9,10},{10,1... | collective-permute-start | bytes 884744 | tf_op jit(solution)/shard_map/ppermute | solution.py:64
  547.7 8.7 %collective-permute-start.2 = (f32[192,384]{1,0:T(8,128)S(1)}, f32[192,384]{1,0:T(8,128)S(1)}, u32[]{:S(2)}, u32[]{:S(2)}) collective-permute-start(f32[192,384]{1,0:T(8,128)S(1)} %collective-permute-done.1), channel_id=1, source_target_pairs={{0,1},{1,2},{2,3},{3,0},{4,5},{5,6},{6,7},{7,4},{8,9},{9,10},{10,1... | collective-permute-start | bytes 884744 | tf_op jit(solution)/shard_map/ppermute | solution.py:64
  582.6 61.6 %copy-start.3 = (f32[192,256]{1,0:T(8,128)S(1)}, f32[192,256]{1,0:T(8,128)}, u32[]{:S(2)}) copy-start(f32[192,256]{1,0:T(8,128)} %constant_dynamic-slice_fusion.1) | copy-start | bytes 589828
  619.5 28.0 %copy-start.1 = (bf16[48,32,256]{2,1,0:T(8,128)(2,1)S(1)}, bf16[48,32,256]{2,1,0:T(8,128)(2,1)}, u32[]{:S(2)}) copy-start(bf16[48,32,256]{2,1,0:T(8,128)(2,1)} %param.6) | copy-start | bytes 2359300
  644.6 2.9 copy-start.4
Sparse Core Ops, SparseCore 0:
  411.9 83.0 reduce-scatter.6
  497.4 29.1 reduce-scatter.4
  557.8 23.8 all-gather.1
